TPU v7x, 256 devices: a whole 4x4x8 slice. The times are simulated.
256 devices in a mesh: lat: 4 (over y_hi, core), lon: 64 (over y_lo, z, x).
Axes of the slice: x: 4, y: 4 (y_hi: 2, y_lo: 2; y = y_hi * 2 + y_lo), z: 8, core: 2. Of those that a mesh axis runs over, the one named last changes fastest.
Arguments:
- inputs: bfloat16 [8, 24, 768, 192], P(None, 'lat', 'lon'), may hold values from -6 to 6
- cotangent: bfloat16 [8, 24, 768, 192], P(None, 'lat', 'lon'), may hold values from -6 to 6
- qkv_weight: bfloat16 [192, 576], P(None, 'lon'), may hold values from -0.4375 to 0.4375
- proj_weight: bfloat16 [192, 192], P(None, 'lon'), may hold values from -0.4375 to 0.4375
- up_weight: bfloat16 [192, 768], P(None, 'lon'), may hold values from -0.4375 to 0.4375
- down_weight: bfloat16 [768, 192], P(None, 'lon'), may hold values from -0.21875 to 0.21875
- norm_gains: bfloat16 [2, 192], P(None, 'lon'), may hold values from 0.099609375 to 1.8984375
- bias_table: bfloat16 [16, 6, 20736], P(None, None, 'lon'), may hold values from -4 to 304
- type_of: int32 [4, 4], replicated, may hold values from 0 to 15
- region: int32 [8, 24], P(None, 'lat'), may hold values from 0 to 2
Outputs:
- grad_input: bfloat16 [8, 24, 768, 192], P(None, 'lat', 'lon')
- grad_qkv: float32 [192, 576], P(None, 'lon')
- grad_proj: float32 [192, 192], P(None, 'lon')
- grad_up: float32 [192, 768], P(None, 'lon')
- grad_down: float32 [768, 192], P(None, 'lon')
- grad_gains: float32 [2, 192], P(None, 'lon')
- grad_table: float32 [16, 6, 20736], P(None, None, 'lon')
Inputs may be any that keep to these rules, and one draw needn't show every extreme that they name: `type_of`: types may repeat and some may be absent. Attention joins only tokens of a window with equal region ids.
All inputs are finite; a program needn't handle non-finite values.
Results may differ from a plain program's by a relative error of at most 0.015.
Values may be sent and summed in bfloat16 or wider, within the bound.
No kernel may reach another device: no remote copies, remote signals or barrier semaphores. Data moves between devices by JAX's collectives and lax.ppermute only.
A program may use at most 64 MiB of HBM per device.

v0:
```python
import math
import jax
import jax.numpy as jnp
from jax import lax
from jax.sharding import PartitionSpec as P

WPL = 2
WLAT = 6
WLON = 12
WIN = 144


def passed_along(block, axis, distance):
    devices = range(lax.axis_size(axis))
    route = [((i - distance) % len(devices), i) for i in devices]
    return lax.ppermute(block, axis, route)


def layer_norm(values):
    row_mean = jnp.mean(values, axis=-1, keepdims=True)
    centred = values - row_mean
    variance = jnp.mean(centred * centred, axis=-1, keepdims=True)
    inv_std = lax.rsqrt(variance + 1e-05)
    return (centred * inv_std, inv_std)


def norm_back(d_normed, normed, inv_std):
    return inv_std * (
        d_normed
        - jnp.mean(d_normed, axis=-1, keepdims=True)
        - normed * jnp.mean(d_normed * normed, axis=-1, keepdims=True)
    )


def gelu_pair(pre_act):
    cumul = 0.5 * (1.0 + lax.erf(pre_act * 0.7071067811865476))
    density = jnp.exp(-0.5 * pre_act * pre_act) * 0.3989422804014327
    return (pre_act * cumul, cumul + pre_act * density)


def to_windows(column, level_windows, row_windows):
    features = column.shape[-1]
    shaped = column.reshape(level_windows, WPL, row_windows, WLAT, WLON, features)
    return shaped.transpose(0, 2, 1, 3, 4, 5).reshape(level_windows * row_windows * WIN, features)


def from_windows(flat, level_windows, row_windows):
    features = flat.shape[-1]
    shaped = flat.reshape(level_windows, row_windows, WPL, WLAT, WLON, features)
    return shaped.transpose(0, 2, 1, 3, 4, 5).reshape(
        level_windows * WPL, row_windows * WLAT, WLON, features
    )


def region_mask(region_rows, level_windows, row_windows):
    labels = region_rows.reshape(level_windows, WPL, row_windows, WLAT).transpose(0, 2, 1, 3)
    labels = jnp.broadcast_to(labels[..., None], (level_windows, row_windows, WPL, WLAT, WLON))
    labels = labels.reshape(level_windows, row_windows, WIN)
    return labels[..., :, None] == labels[..., None, :]


def roll_block(stacked, forward):
    level_shift = WPL // 2
    stacked = jnp.roll(stacked, -level_shift if forward else level_shift, axis=1)
    row_half = WLAT // 2
    rim_rows = stacked[:, :, :row_half] if forward else stacked[:, :, -row_half:]
    arrived = passed_along(rim_rows, "lat", -1 if forward else 1)
    if forward:
        stacked = jnp.concatenate([stacked[:, :, row_half:], arrived], axis=2)
    else:
        stacked = jnp.concatenate([arrived, stacked[:, :, :-row_half]], axis=2)
    col_half = WLON // 2
    rim_cols = stacked[:, :, :, :col_half] if forward else stacked[:, :, :, -col_half:]
    landed = passed_along(rim_cols, "lon", -1 if forward else 1)
    if forward:
        stacked = jnp.concatenate([stacked[:, :, :, col_half:], landed], axis=3)
    else:
        stacked = jnp.concatenate([landed, stacked[:, :, :, :-col_half]], axis=3)
    return stacked


def column_grads(column, cot_column, weights, bias_pos, same_region):
    qkv_full, proj_full, up_full, down_full, gains_full = weights
    f32 = jnp.float32
    bf16 = jnp.bfloat16
    level_windows = column.shape[0] // WPL
    row_windows = column.shape[1] // WLAT
    features = column.shape[-1]
    head_count = bias_pos.shape[2]
    head_size = features // head_count
    factor = 1.0 / math.sqrt(head_size)
    gain_one = gains_full[0].astype(f32)
    gain_two = gains_full[1].astype(f32)
    window_cells = to_windows(column, level_windows, row_windows).astype(f32)
    normed_one, inv_one = layer_norm(window_cells)
    scaled_one = (normed_one * gain_one).astype(bf16)
    packed = jnp.dot(scaled_one, qkv_full, preferred_element_type=f32).astype(bf16)
    packed = packed.reshape(level_windows, row_windows, WIN, 3, head_count, head_size)
    queries = packed[:, :, :, 0]
    key_rows = packed[:, :, :, 1]
    value_rows = packed[:, :, :, 2]
    scores = (
        jnp.einsum("abthd,abshd->abhts", queries, key_rows, preferred_element_type=f32) * factor
    )
    scores = scores + bias_pos.astype(f32)
    scores = jnp.where(same_region[:, :, None], scores, -jnp.inf)
    peak_score = jnp.max(scores, axis=-1, keepdims=True)
    raised = jnp.exp(scores - peak_score)
    attn_probs = raised / jnp.sum(raised, axis=-1, keepdims=True)
    probs_b = attn_probs.astype(bf16)
    attended = jnp.einsum("abhts,abshd->abthd", probs_b, value_rows, preferred_element_type=f32)
    attended = attended.astype(bf16).reshape(-1, features)
    middle = window_cells + jnp.dot(attended, proj_full, preferred_element_type=f32)
    normed_two, inv_two = layer_norm(middle)
    scaled_two = (normed_two * gain_two).astype(bf16)
    pre_act = jnp.dot(scaled_two, up_full, preferred_element_type=f32)
    activated, gelu_slope = gelu_pair(pre_act)
    hidden_b = activated.astype(bf16)
    cot_rows = to_windows(cot_column, level_windows, row_windows)
    grad_down = jnp.dot(hidden_b.T, cot_rows, preferred_element_type=f32)
    d_hidden = (jnp.dot(cot_rows, down_full.T, preferred_element_type=f32) * gelu_slope).astype(
        bf16
    )
    grad_up = jnp.dot(scaled_two.T, d_hidden, preferred_element_type=f32)
    d_htwo = jnp.dot(d_hidden, up_full.T, preferred_element_type=f32)
    gain_grad_two = jnp.sum(d_htwo * normed_two, axis=0)
    d_middle = cot_rows.astype(f32) + norm_back(d_htwo * gain_two, normed_two, inv_two)
    d_middle_b = d_middle.astype(bf16)
    grad_proj = jnp.dot(attended.T, d_middle_b, preferred_element_type=f32)
    d_att = jnp.dot(d_middle_b, proj_full.T, preferred_element_type=f32).astype(bf16)
    d_att = d_att.reshape(level_windows, row_windows, WIN, head_count, head_size)
    d_prob = jnp.einsum("abthd,abshd->abhts", d_att, value_rows, preferred_element_type=f32)
    d_values = jnp.einsum("abhts,abthd->abshd", probs_b, d_att, preferred_element_type=f32)
    d_score = attn_probs * (d_prob - jnp.sum(attn_probs * d_prob, axis=-1, keepdims=True))
    d_score_b = d_score.astype(bf16)
    d_queries = (
        jnp.einsum("abhts,abshd->abthd", d_score_b, key_rows, preferred_element_type=f32) * factor
    )
    d_keys = (
        jnp.einsum("abhts,abthd->abshd", d_score_b, queries, preferred_element_type=f32) * factor
    )
    d_packed = (
        jnp.stack([d_queries, d_keys, d_values], axis=3).astype(bf16).reshape(-1, 3 * features)
    )
    grad_qkv = jnp.dot(scaled_one.T, d_packed, preferred_element_type=f32)
    d_hone = jnp.dot(d_packed, qkv_full.T, preferred_element_type=f32)
    gain_grad_one = jnp.sum(d_hone * normed_one, axis=0)
    d_cells = d_middle + norm_back(d_hone * gain_one, normed_one, inv_one)
    d_column = from_windows(d_cells.astype(bf16), level_windows, row_windows)
    param_grads = (
        grad_qkv,
        grad_proj,
        grad_up,
        grad_down,
        jnp.stack([gain_grad_one, gain_grad_two]),
    )
    table_grad = d_score.reshape(level_windows * row_windows, head_count, WIN * WIN)
    return (d_column, param_grads, table_grad)


def shards(
    inputs,
    cotangent,
    qkv_weight,
    proj_weight,
    up_weight,
    down_weight,
    norm_gains,
    bias_table,
    type_of,
    region,
):
    level_windows = inputs.shape[0] // WPL
    row_windows = inputs.shape[1] // WLAT
    lon_windows = inputs.shape[2] // WLON
    features = inputs.shape[3]
    type_count = bias_table.shape[0]
    head_count = bias_table.shape[1]
    positions = level_windows * row_windows
    lat_index = lax.axis_index("lat")
    type_rows = lax.dynamic_slice(
        type_of, (jnp.int32(0), lat_index * row_windows), (level_windows, row_windows)
    ).reshape(-1)
    onehot = type_rows[:, None] == jnp.arange(type_count, dtype=jnp.int32)[None, :]
    select_half = onehot.astype(jnp.bfloat16)
    select_full = onehot.astype(jnp.float32)
    table_part = bias_table.reshape(type_count * head_count, -1)
    qkv_full, proj_full, up_full, down_full, gains_full, table_full = (
        lax.all_gather(qkv_weight, "lon", axis=1, tiled=True),
        lax.all_gather(proj_weight, "lon", axis=1, tiled=True),
        lax.all_gather(up_weight, "lon", axis=1, tiled=True),
        lax.all_gather(down_weight, "lon", axis=1, tiled=True),
        lax.all_gather(norm_gains, "lon", axis=1, tiled=True),
        lax.all_gather(table_part, "lon", axis=1, tiled=True),
    )
    chosen_rows = jnp.dot(
        select_half, table_full.reshape(type_count, -1), preferred_element_type=jnp.float32
    )
    bias_pos = chosen_rows.astype(jnp.bfloat16).reshape(
        level_windows, row_windows, head_count, WIN, WIN
    )
    same_region = region_mask(region, level_windows, row_windows)
    shifted = roll_block(jnp.stack([inputs, cotangent]), True)
    columns = shifted.reshape(2, inputs.shape[0], inputs.shape[1], lon_windows, WLON, features)
    columns = columns.transpose(3, 0, 1, 2, 4, 5)
    weights = (qkv_full, proj_full, up_full, down_full, gains_full)

    def advance(totals, column_pair):
        d_column, param_grads, table_grad = column_grads(
            column_pair[0], column_pair[1], weights, bias_pos, same_region
        )
        return (jax.tree.map(jnp.add, totals, (param_grads, table_grad)), d_column)

    initial = (
        tuple((jnp.zeros(member.shape, jnp.float32) for member in weights)),
        jnp.zeros((positions, head_count, WIN * WIN), jnp.float32),
    )
    totals, d_columns = lax.scan(advance, initial, columns)
    d_shifted = d_columns.transpose(1, 2, 0, 3, 4).reshape(inputs.shape)
    grad_input = roll_block(d_shifted[None], False)[0]
    param_grads, table_sum = totals
    table_member = jnp.dot(
        select_full.T, table_sum.reshape(positions, -1), precision=lax.Precision.HIGHEST
    ).reshape(type_count * head_count, -1)
    summed = (
        lax.psum_scatter(param_grads[0], "lon", scatter_dimension=1, tiled=True),
        lax.psum_scatter(param_grads[1], "lon", scatter_dimension=1, tiled=True),
        lax.psum_scatter(param_grads[2], "lon", scatter_dimension=1, tiled=True),
        lax.psum_scatter(param_grads[3], "lon", scatter_dimension=1, tiled=True),
        lax.psum_scatter(param_grads[4], "lon", scatter_dimension=1, tiled=True),
        lax.psum_scatter(table_member, "lon", scatter_dimension=1, tiled=True),
    )
    table_shard = summed[5]
    lat_sums = (
        lax.psum(summed[0].astype(jnp.bfloat16), "lat").astype(jnp.float32),
        lax.psum(summed[1].astype(jnp.bfloat16), "lat").astype(jnp.float32),
        lax.psum(summed[2].astype(jnp.bfloat16), "lat").astype(jnp.float32),
        lax.psum(summed[3].astype(jnp.bfloat16), "lat").astype(jnp.float32),
        lax.psum(summed[4].astype(jnp.bfloat16), "lat").astype(jnp.float32),
        lax.psum(table_shard.astype(jnp.bfloat16), "lat").astype(jnp.float32),
    )
    token_count = (
        inputs.shape[0]
        * inputs.shape[1]
        * inputs.shape[2]
        * lax.axis_size("lat")
        * lax.axis_size("lon")
    )
    factor = 1.0 / math.sqrt(token_count)
    return (
        grad_input,
        lat_sums[0] * factor,
        lat_sums[1] * factor,
        lat_sums[2] * factor,
        lat_sums[3] * factor,
        lat_sums[4] * factor,
        lat_sums[5].reshape(type_count, head_count, -1),
    )


def solution(mesh):
    return jax.shard_map(
        shards,
        mesh=mesh,
        in_specs=(
            P(None, "lat", "lon", None),
            P(None, "lat", "lon", None),
            P(None, "lon"),
            P(None, "lon"),
            P(None, "lon"),
            P(None, "lon"),
            P(None, "lon"),
            P(None, None, "lon"),
            P(),
            P(None, "lat"),
        ),
        out_specs=(
            P(None, "lat", "lon", None),
            P(None, "lon"),
            P(None, "lon"),
            P(None, "lon"),
            P(None, "lon"),
            P(None, "lon"),
            P(None, None, "lon"),
        ),
        check_vma=False,
    )
```

profile of v0, /device:TPU:1, one launch (start us, length us, event | category | flops | bytes accessed | tf_op | source)
XLA Modules:
  0.0 1554.6 jit_solution(2564097191101022794)
XLA Ops:
  17.5 131.0 %all-gather = bf16[64,3,2]{1,2,0:T(2,128)(2,1)S(1)} all-gather(bf16[1,3,2]{1,2,0:T(2,128)(2,1)S(1)} %bitcast.129), channel_id=1, replica_groups=mesh['lat'=4,'lon'=64] {'lon'}, dimensions={0}, use_global_device_ids=true | all-gather | bytes 780 | tf_op jit(solution)/shard_map/all_gather | solution.py:193
  148.9 127.0 %all-gather.3 = bf16[64,3,192]{2,1,0:T(4,128)(2,1)S(1)} all-gather(bf16[1,3,192]{2,1,0:T(4,128)(2,1)S(1)} %bitcast.127), channel_id=1, replica_groups=mesh['lat'=4,'lon'=64] {'lon'}, dimensions={0}, use_global_device_ids=true | all-gather | bytes 74880 | tf_op jit(solution)/shard_map/all_gather | solution.py:190
  276.6 127.6 %all-gather.4 = bf16[64,3,768]{2,1,0:T(4,128)(2,1)S(1)} all-gather(bf16[1,3,768]{2,1,0:T(4,128)(2,1)S(1)} %bitcast.124), channel_id=1, replica_groups=mesh['lat'=4,'lon'=64] {'lon'}, dimensions={0}, use_global_device_ids=true | all-gather | bytes 299520 | tf_op jit(solution)/shard_map/all_gather | solution.py:192
  405.1 124.9 %all-gather.1 = bf16[64,9,192]{2,1,0:T(8,128)(2,1)S(1)} all-gather(bf16[1,9,192]{2,1,0:T(8,128)(2,1)S(1)} %bitcast.122), channel_id=1, replica_groups=mesh['lat'=4,'lon'=64] {'lon'}, dimensions={0}, use_global_device_ids=true | all-gather | bytes 224640 | tf_op jit(solution)/shard_map/all_gather | solution.py:189
  530.2 126.4 %all-gather.5 = bf16[64,12,192]{2,1,0:T(8,128)(2,1)S(1)} all-gather(bf16[1,12,192]{2,1,0:T(8,128)(2,1)S(1)} %bitcast.123), channel_id=1, replica_groups=mesh['lat'=4,'lon'=64] {'lon'}, dimensions={0}, use_global_device_ids=true | all-gather | bytes 299520 | tf_op jit(solution)/shard_map/all_gather | solution.py:191
  659.7 5.6 collective-permute-done.1
  672.1 6.3 copy.70
  678.4 9.6 reshape.312
  688.0 7.4 reshape.296
  695.5 4.2 fusion.2
  699.6 4.7 reshape.305
  704.4 3.6 copy.71
  724.9 134.0 %fusion = f32[192,16]{0,1:T(8,128)S(1)} fusion(f32[192,768]{0,1:T(8,128)S(1)} %fusion.35), kind=kCustom, calls=%all-reduce-scatter | all-reduce-scatter fusion | flops 196609 | bytes 603136
  870.1 5.0 convolution_bitcast_fusion
  885.9 4.7 reshape.299
  900.0 5.8 fusion.31
  905.9 6.2 reshape.300
  912.1 314.7 %all-reduce.13 = (bf16[96,20736]{1,0:T(8,128)(2,1)}, bf16[192,576]{0,1:T(8,128)(2,1)S(1)}, bf16[192,192]{0,1:T(8,128)(2,1)S(1)}, bf16[768,192]{0,1:T(8,128)(2,1)}, bf16[2,192]{1,0:T(2,128)(2,1)S(1)}) all-reduce(f32[96,20736]{1,0:T(8,128)} %reshape.300, ...), channel_id=7, replica_groups=mesh['lat'=4,'lon'=64] {'lon'}, use_global_device_ids=true, to_apply=%region_23.24.clone | all-reduce | flops 2285952 | bytes 13715712
  1233.8 17.3 %collective-permute-start.12 = (bf16[192,16]{0,1:T(8,128)(2,1)}, bf16[192,16]{0,1:T(8,128)(2,1)S(1)}, u32[]{:S(2)}, u32[]{:S(2)}) collective-permute-start(bf16[192,16]{0,1:T(8,128)(2,1)} %convert.35), channel_id=1, source_target_pairs={{0,9},{1,10},{2,11},{3,12},{4,13},{5,14},{6,15},{7,16},{8,17},{9,1... | collective-permute-start | bytes 18440
  1251.2 6.6 collective-permute-start.13
  1271.9 4.6 concatenate.34
  1277.1 213.3 %collective-permute-start.2 = (bf16[1,8,3,12,192]{4,3,2,1,0:T(8,128)(2,1)S(1)}, bf16[1,8,3,12,192]{4,3,2,1,0:T(8,128)(2,1)S(1)}, u32[]{:S(2)}, u32[]{:S(2)}) collective-permute-start(bf16[1,8,3,12,192]{4,3,2,1,0:T(8,128)(2,1)S(1)} %fusion.27), channel_id=1, source_target_pairs={{192,0},{0,64},{64,128},{128,192},{193,1},{1,65},{65,129},{129,193... | collective-permute-start | bytes 331784 | tf_op jit(solution)/shard_map/ppermute | solution.py:16
  1490.4 39.8 %all-reduce.12.cloned.1.call-done = (bf16[16,6,324]{2,1,0:T(8,128)(2,1)}, bf16[192,9]{0,1:T(8,128)(2,1)}, bf16[192,3]{0,1:T(4,128)(2,1)}, bf16[192,12]{0,1:T(8,1...) async-done(((bf16[16,6,324]{2,1,0:T(8,128)(2,1)}, bf16[192,9]{0,1:T(8,128)(2,1)}, bf16[192,3]{0,1:T(4,128)(2,1)}, bf16[192,12]{0,1:T(8,128)(2,1)}, ...) | async-done | bytes 76060 | tf_op jit(solution)/shard_map/psum | solution.py:240
  1539.6 6.7 collective-permute-done.3
  (217 shorter events, 99.6 us)
Async XLA Ops:
  7.2 651.1 %copy-start = (s32[4,4]{1,0:T(4,128)S(1)}, s32[4,4]{1,0:T(4,128)}, u32[]{:S(2)}) copy-start(s32[4,4]{1,0:T(4,128)} %param.18) | copy-start | bytes 196
  7.2 664.9 %all-gather.8.cloned.1.call-start = ((), (), s32[]{:S(2)}) async-start(), calls=%async_computation | async-start | bytes 4792320 | tf_op jit(solution)/shard_map/all_gather | solution.py:194
  8.9 1521.3 %all-reduce.12.cloned.1.call-start = ((), (), s32[]{:S(2)}) async-start(), calls=%async_computation.1 | async-start | bytes 246784 | tf_op jit(solution)/shard_map/psum | solution.py:240
  9.0 521.3 %copy-start.31 = (bf16[192,12]{0,1:T(8,128)(2,1)S(1)}, bf16[192,12]{0,1:T(8,128)(2,1)}, u32[]{:S(2)}) copy-start(bf16[192,12]{0,1:T(8,128)(2,1)} %param.14) | copy-start | bytes 13828
  11.6 647.7 %collective-permute-start = (bf16[2,8,3,12,192]{4,1,3,2,0:T(8,128)(2,1)S(1)}, bf16[2,8,3,12,192]{4,1,3,2,0:T(8,128)(2,1)S(1)}, u32[]{:S(2)}, u32[]{:S(2)}) collective-permute-start(bf16[2,8,3,12,192]{4,1,3,2,0:T(8,128)(2,1)S(1)} %get-tuple-element.93), channel_id=1, source_target_pairs={{64,0},{128,64},{192,128},{0,192},{65,1},{129,65},{193,129},{1,193... | collective-permute-start | bytes 663560 | tf_op jit(solution)/shard_map/ppermute | solution.py:16
  659.4 5.9 collective-permute-start.1
  860.1 371.1 %collective-permute-start.5 = (bf16[192,16]{0,1:T(8,128)(2,1)}, bf16[192,16]{0,1:T(8,128)(2,1)}, u32[]{:S(2)}, u32[]{:S(2)}) collective-permute-start(bf16[192,16]{0,1:T(8,128)(2,1)} %convert.35), channel_id=1, source_target_pairs={{0,2},{1,3},{2,4},{3,5},{4,6},{5,7},{6,8},{7,9},{8,10},{9,11},{10,... | collective-permute-start | bytes 18440
  862.0 370.5 %collective-permute-start.6 = (bf16[192,16]{0,1:T(8,128)(2,1)}, bf16[192,16]{0,1:T(8,128)(2,1)}, u32[]{:S(2)}, u32[]{:S(2)}) collective-permute-start(bf16[192,16]{0,1:T(8,128)(2,1)} %convert.35), channel_id=1, source_target_pairs={{0,3},{1,4},{2,5},{3,6},{4,7},{5,8},{6,9},{7,10},{8,11},{9,12},{10... | collective-permute-start | bytes 18440
  863.9 370.0 %collective-permute-start.7 = (bf16[192,16]{0,1:T(8,128)(2,1)}, bf16[192,16]{0,1:T(8,128)(2,1)}, u32[]{:S(2)}, u32[]{:S(2)}) collective-permute-start(bf16[192,16]{0,1:T(8,128)(2,1)} %convert.35), channel_id=1, source_target_pairs={{0,4},{1,5},{2,6},{3,7},{4,8},{5,9},{6,10},{7,11},{8,12},{9,13},{1... | collective-permute-start | bytes 18440
  865.7 385.5 %collective-permute-start.8 = (bf16[192,16]{0,1:T(8,128)(2,1)}, bf16[192,16]{0,1:T(8,128)(2,1)}, u32[]{:S(2)}, u32[]{:S(2)}) collective-permute-start(bf16[192,16]{0,1:T(8,128)(2,1)} %convert.35), channel_id=1, source_target_pairs={{0,5},{1,6},{2,7},{3,8},{4,9},{5,10},{6,11},{7,12},{8,13},{9,14},{... | collective-permute-start | bytes 18440
  884.3 344.3 %collective-permute-start.19 = (bf16[192,12]{0,1:T(8,128)(2,1)}, bf16[192,12]{0,1:T(8,128)(2,1)S(1)}, u32[]{:S(2)}, u32[]{:S(2)}) collective-permute-start(bf16[192,12]{0,1:T(8,128)(2,1)} %slice.107), channel_id=1, source_target_pairs={{0,16},{1,17},{2,18},{3,19},{4,20},{5,21},{6,22},{7,23},{8,24},{9,... | collective-permute-start | bytes 13832
  1228.6 29.2 %collective-permute-start.9 = (bf16[192,16]{0,1:T(8,128)(2,1)}, bf16[192,16]{0,1:T(8,128)(2,1)S(1)}, u32[]{:S(2)}, u32[]{:S(2)}) collective-permute-start(bf16[192,16]{0,1:T(8,128)(2,1)} %convert.35), channel_id=1, source_target_pairs={{0,6},{1,7},{2,8},{3,9},{4,10},{5,11},{6,12},{7,13},{8,14},{9,15},... | collective-permute-start | bytes 18440
  1231.2 28.4 %collective-permute-start.10 = (bf16[192,16]{0,1:T(8,128)(2,1)}, bf16[192,16]{0,1:T(8,128)(2,1)S(1)}, u32[]{:S(2)}, u32[]{:S(2)}) collective-permute-start(bf16[192,16]{0,1:T(8,128)(2,1)} %convert.35), channel_id=1, source_target_pairs={{0,7},{1,8},{2,9},{3,10},{4,11},{5,12},{6,13},{7,14},{8,15},{9,16}... | collective-permute-start | bytes 18440
  1232.5 28.4 %collective-permute-start.11 = (bf16[192,16]{0,1:T(8,128)(2,1)}, bf16[192,16]{0,1:T(8,128)(2,1)S(1)}, u32[]{:S(2)}, u32[]{:S(2)}) collective-permute-start(bf16[192,16]{0,1:T(8,128)(2,1)} %convert.35), channel_id=1, source_target_pairs={{0,8},{1,9},{2,10},{3,11},{4,12},{5,13},{6,14},{7,15},{8,16},{9,17... | collective-permute-start | bytes 18440
  1233.8 29.2 %collective-permute-start.12 = (bf16[192,16]{0,1:T(8,128)(2,1)}, bf16[192,16]{0,1:T(8,128)(2,1)S(1)}, u32[]{:S(2)}, u32[]{:S(2)}) collective-permute-start(bf16[192,16]{0,1:T(8,128)(2,1)} %convert.35), channel_id=1, source_target_pairs={{0,9},{1,10},{2,11},{3,12},{4,13},{5,14},{6,15},{7,16},{8,17},{9,1... | collective-permute-start | bytes 18440
  1251.2 13.7 collective-permute-start.13
  1257.8 9.7 collective-permute-start.14
  1259.7 12.1 collective-permute-start.15
  1261.0 10.8 collective-permute-start.16
  1263.0 8.8 collective-permute-start.17
  1265.0 6.9 collective-permute-start.18
  1267.5 4.3 collective-permute-start.4
  1277.1 258.3 %collective-permute-start.2 = (bf16[1,8,3,12,192]{4,3,2,1,0:T(8,128)(2,1)S(1)}, bf16[1,8,3,12,192]{4,3,2,1,0:T(8,128)(2,1)S(1)}, u32[]{:S(2)}, u32[]{:S(2)}) collective-permute-start(bf16[1,8,3,12,192]{4,3,2,1,0:T(8,128)(2,1)S(1)} %fusion.27), channel_id=1, source_target_pairs={{192,0},{0,64},{64,128},{128,192},{193,1},{1,65},{65,129},{129,193... | collective-permute-start | bytes 331784 | tf_op jit(solution)/shard_map/ppermute | solution.py:16
  1535.6 10.7 collective-permute-start.3
  (38 other events, 2545.0 us)
Sparse Core Ops, SparseCore 0:
  9.9 267.2 all-gather.7
  1277.2 253.0 all-reduce.11
where the time goes:
time: 1560 us; the launch traced here: 1550 us
  blocking collectives  1090 us (70%)
  starting transfers between devices  267 us (17%)
  local copies, waits for them, and re-layouts  77.9 us (5%)
  waiting for transfers between devices  52.2 us (3%)
  matrix products  36.5 us (2%)
  between operations  18 us (1%)
  other arithmetic  17.4 us (1%)
    unnamed x2, blocking collectives  449 us
    ppermute x4, starting transfers between devices, passed_along(): return lax.ppermute(block, axis, route)  218 us
    all_gather x1, blocking collectives, shards(): lax.all_gather(norm_gains, 'lon', axis=1, tiled=True)  131 us
    all_gather x1, blocking collectives, shards(): lax.all_gather(down_weight, 'lon', axis=1, tiled=True)  128 us
    all_gather x1, blocking collectives, shards(): lax.all_gather(proj_weight, 'lon', axis=1, tiled=True)  127 us
    all_gather x1, blocking collectives, shards(): lax.all_gather(up_weight, 'lon', axis=1, tiled=True)  126 us
    all_gather x1, blocking collectives, shards(): lax.all_gather(qkv_weight, 'lon', axis=1, tiled=True)  125 us
    unnamed x16, starting transfers between devices  48.6 us
  transfers between devices with their start and end apart: 22, of which 3 were waited for; matrix products, arithmetic and copies ran while one was open for 4% of the time, Pallas kernels for 0%

commit v1 on v0

--- a/solution.py
+++ b/solution.py
@@ -8,6 +8,11 @@
 WLAT = 6
 WLON = 12
 WIN = 144
+
+
+def all_by_exchange(x, name, dim):
+    outgoing = jnp.stack([x] * lax.axis_size(name))
+    return jnp.concatenate(lax.all_to_all(outgoing, name, 0, 0), axis=dim)
 
 
 def passed_along(block, axis, distance):
@@ -187,7 +192,7 @@
     table_part = bias_table.reshape(type_count * head_count, -1)
     qkv_full, proj_full, up_full, down_full, gains_full, table_full = (
         lax.all_gather(qkv_weight, "lon", axis=1, tiled=True),
-        lax.all_gather(proj_weight, "lon", axis=1, tiled=True),
+        all_by_exchange(proj_weight, "lon", 1),
         lax.all_gather(up_weight, "lon", axis=1, tiled=True),
         lax.all_gather(down_weight, "lon", axis=1, tiled=True),
         lax.all_gather(norm_gains, "lon", axis=1, tiled=True),

time: 1560 us -> 1430 us (0.917)
  blocking collectives: 1090 us -> 959 us
    all_gather x1 -> x0, blocking collectives: 127 us -> none  [shards(): lax.all_gather(proj_weight, 'lon', axis=1, tiled=True)]
    ppermute x4, starting transfers between devices: 218 us -> 189 us  [passed_along(): return lax.ppermute(block, axis, route)]
  transfers between devices with their start and end apart: 22 -> 23, of which waited for: 3 -> 3; matrix products, arithmetic and copies ran while one was open for 4% -> 5% of each run, Pallas kernels for 0% -> 0%
where the time goes in v1:
time: 1430 us; the launch traced here: 1420 us
  blocking collectives  959 us (67%)
  starting transfers between devices  254 us (18%)
  local copies, waits for them, and re-layouts  79.3 us (6%)
  waiting for transfers between devices  50.9 us (4%)
  matrix products  36.6 us (3%)
  between operations  18 us (1%)
  other arithmetic  17.5 us (1%)
    unnamed x2, blocking collectives  448 us
    ppermute x4, starting transfers between devices, passed_along(): return lax.ppermute(block, axis, route)  189 us
    all_gather x1, blocking collectives, shards(): lax.all_gather(norm_gains, 'lon', axis=1, tiled=True)  129 us
    all_gather x1, blocking collectives, shards(): lax.all_gather(down_weight, 'lon', axis=1, tiled=True)  129 us
    all_gather x1, blocking collectives, shards(): lax.all_gather(qkv_weight, 'lon', axis=1, tiled=True)  127 us
    all_gather x1, blocking collectives, shards(): lax.all_gather(up_weight, 'lon', axis=1, tiled=True)  126 us
    unnamed x16, starting transfers between devices  51.2 us
    psum x1, waiting for transfers between devices, shards(): lax.psum(table_shard.astype(jnp.bfloat16), 'lat').astype(jnp.float32)  39.8 us
  transfers between devices with their start and end apart: 23, of which 3 were waited for; matrix products, arithmetic and copies ran while one was open for 5% of the time, Pallas kernels for 0%

profile of v1, /device:TPU:1, one launch (start us, length us, event | category | flops | bytes accessed | tf_op | source)
XLA Modules:
  0.0 1415.6 jit_solution(18100921978384626069)
XLA Ops:
  10.3 13.6 all-to-all-start
  30.2 129.4 %all-gather = bf16[64,3,2]{1,2,0:T(2,128)(2,1)S(1)} all-gather(bf16[1,3,2]{1,2,0:T(2,128)(2,1)S(1)} %bitcast.129), channel_id=1, replica_groups=mesh['lat'=4,'lon'=64] {'lon'}, dimensions={0}, use_global_device_ids=true | all-gather | bytes 780 | tf_op jit(solution)/shard_map/all_gather | solution.py:198
  159.9 129.1 %all-gather.3 = bf16[64,3,768]{2,1,0:T(4,128)(2,1)S(1)} all-gather(bf16[1,3,768]{2,1,0:T(4,128)(2,1)S(1)} %bitcast.125), channel_id=1, replica_groups=mesh['lat'=4,'lon'=64] {'lon'}, dimensions={0}, use_global_device_ids=true | all-gather | bytes 299520 | tf_op jit(solution)/shard_map/all_gather | solution.py:197
  290.0 126.5 %all-gather.1 = bf16[64,9,192]{2,1,0:T(8,128)(2,1)S(1)} all-gather(bf16[1,9,192]{2,1,0:T(8,128)(2,1)S(1)} %bitcast.123), channel_id=1, replica_groups=mesh['lat'=4,'lon'=64] {'lon'}, dimensions={0}, use_global_device_ids=true | all-gather | bytes 224640 | tf_op jit(solution)/shard_map/all_gather | solution.py:194
  416.8 125.8 %all-gather.4 = bf16[64,12,192]{2,1,0:T(8,128)(2,1)S(1)} all-gather(bf16[1,12,192]{2,1,0:T(8,128)(2,1)S(1)} %bitcast.124), channel_id=1, replica_groups=mesh['lat'=4,'lon'=64] {'lon'}, dimensions={0}, use_global_device_ids=true | all-gather | bytes 299520 | tf_op jit(solution)/shard_map/all_gather | solution.py:196
  546.9 4.3 collective-permute-done.1
  558.0 6.3 copy.71
  564.3 9.6 reshape.322
  573.9 7.4 reshape.304
  585.5 4.7 reshape.315
  610.8 133.8 %fusion = f32[192,16]{0,1:T(8,128)S(1)} fusion(f32[192,768]{0,1:T(8,128)S(1)} %fusion.35), kind=kCustom, calls=%all-reduce-scatter | all-reduce-scatter fusion | flops 196609 | bytes 603136
  755.8 5.0 convolution_bitcast_fusion
  770.0 6.1 collective-permute-start.19
  776.0 4.7 reshape.309
  790.2 5.8 fusion.31
  796.0 6.2 reshape.310
  802.2 314.5 %all-reduce.13 = (bf16[96,20736]{1,0:T(8,128)(2,1)}, bf16[192,576]{0,1:T(8,128)(2,1)S(1)}, bf16[192,192]{0,1:T(8,128)(2,1)S(1)}, bf16[768,192]{0,1:T(8,128)(2,1)}, bf16[2,192]{1,0:T(2,128)(2,1)S(1)}) all-reduce(f32[96,20736]{1,0:T(8,128)} %reshape.310, ...), channel_id=7, replica_groups=mesh['lat'=4,'lon'=64] {'lon'}, use_global_device_ids=true, to_apply=%region_23.24.clone | all-reduce | flops 2285952 | bytes 13715712
  1123.8 8.8 collective-permute-start.12
  1132.6 6.3 collective-permute-start.13
  1140.8 8.9 collective-permute-start.15
  1159.9 4.6 concatenate.34
  1165.2 186.3 %collective-permute-start.2 = (bf16[1,8,3,12,192]{4,3,2,1,0:T(8,128)(2,1)S(1)}, bf16[1,8,3,12,192]{4,3,2,1,0:T(8,128)(2,1)S(1)}, u32[]{:S(2)}, u32[]{:S(2)}) collective-permute-start(bf16[1,8,3,12,192]{4,3,2,1,0:T(8,128)(2,1)S(1)} %fusion.27), channel_id=1, source_target_pairs={{192,0},{0,64},{64,128},{128,192},{193,1},{1,65},{65,129},{129,193... | collective-permute-start | bytes 331784 | tf_op jit(solution)/shard_map/ppermute | solution.py:21
  1351.5 39.8 %all-reduce.12.cloned.1.call-done = (bf16[16,6,324]{2,1,0:T(8,128)(2,1)}, bf16[192,9]{0,1:T(8,128)(2,1)}, bf16[192,3]{0,1:T(4,128)(2,1)}, bf16[192,12]{0,1:T(8,1...) async-done(((bf16[16,6,324]{2,1,0:T(8,128)(2,1)}, bf16[192,9]{0,1:T(8,128)(2,1)}, bf16[192,3]{0,1:T(4,128)(2,1)}, bf16[192,12]{0,1:T(8,128)(2,1)}, ...) | async-done | bytes 76060 | tf_op jit(solution)/shard_map/psum | solution.py:245
  1400.7 6.6 collective-permute-done.3
  (217 shorter events, 103.5 us)
Async XLA Ops:
  7.2 537.0 %copy-start = (s32[4,4]{1,0:T(4,128)S(1)}, s32[4,4]{1,0:T(4,128)}, u32[]{:S(2)}) copy-start(s32[4,4]{1,0:T(4,128)} %param.18) | copy-start | bytes 196
  7.2 550.8 %all-gather.7.cloned.1.call-start = ((), (), s32[]{:S(2)}) async-start(), calls=%async_computation.1 | async-start | bytes 4792320 | tf_op jit(solution)/shard_map/all_gather | solution.py:199
  10.3 535.9 %all-to-all-start = ((bf16[64,192,3]{1,2,0:T(4,128)(2,1)}), bf16[64,192,3]{1,2,0:T(4,128)(2,1)S(1)}, u32[]{:S(2)}, u32[]{:S(2)}) async-start(bf16[64,192,3]{1,2,0:T(4,128)(2,1)} %stack.32), calls=%async_computation | async-start | bytes 262144 | tf_op jit(solution)/shard_map/all_to_all | solution.py:15
  23.9 1367.4 %all-reduce.12.cloned.1.call-start = ((), (), s32[]{:S(2)}) async-start(), calls=%async_computation.2 | async-start | bytes 246784 | tf_op jit(solution)/shard_map/psum | solution.py:245
  26.6 518.6 %collective-permute-start = (bf16[2,8,3,12,192]{4,1,3,2,0:T(8,128)(2,1)S(1)}, bf16[2,8,3,12,192]{4,1,3,2,0:T(8,128)(2,1)S(1)}, u32[]{:S(2)}, u32[]{:S(2)}) collective-permute-start(bf16[2,8,3,12,192]{4,1,3,2,0:T(8,128)(2,1)S(1)} %get-tuple-element.93), channel_id=1, source_target_pairs={{64,0},{128,64},{192,128},{0,192},{65,1},{129,65},{193,129},{1,193... | collective-permute-start | bytes 663560 | tf_op jit(solution)/shard_map/ppermute | solution.py:21
  545.3 5.9 collective-permute-start.1
  745.8 375.4 %collective-permute-start.5 = (bf16[192,16]{0,1:T(8,128)(2,1)}, bf16[192,16]{0,1:T(8,128)(2,1)}, u32[]{:S(2)}, u32[]{:S(2)}) collective-permute-start(bf16[192,16]{0,1:T(8,128)(2,1)} %convert.35), channel_id=1, source_target_pairs={{0,2},{1,3},{2,4},{3,5},{4,6},{5,7},{6,8},{7,9},{8,10},{9,11},{10,... | collective-permute-start | bytes 18440
  747.7 374.8 %collective-permute-start.6 = (bf16[192,16]{0,1:T(8,128)(2,1)}, bf16[192,16]{0,1:T(8,128)(2,1)}, u32[]{:S(2)}, u32[]{:S(2)}) collective-permute-start(bf16[192,16]{0,1:T(8,128)(2,1)} %convert.35), channel_id=1, source_target_pairs={{0,3},{1,4},{2,5},{3,6},{4,7},{5,8},{6,9},{7,10},{8,11},{9,12},{10... | collective-permute-start | bytes 18440
  749.6 374.2 %collective-permute-start.7 = (bf16[192,16]{0,1:T(8,128)(2,1)}, bf16[192,16]{0,1:T(8,128)(2,1)}, u32[]{:S(2)}, u32[]{:S(2)}) collective-permute-start(bf16[192,16]{0,1:T(8,128)(2,1)} %convert.35), channel_id=1, source_target_pairs={{0,4},{1,5},{2,6},{3,7},{4,8},{5,9},{6,10},{7,11},{8,12},{9,13},{1... | collective-permute-start | bytes 18440
  751.4 381.2 %collective-permute-start.8 = (bf16[192,16]{0,1:T(8,128)(2,1)}, bf16[192,16]{0,1:T(8,128)(2,1)}, u32[]{:S(2)}, u32[]{:S(2)}) collective-permute-start(bf16[192,16]{0,1:T(8,128)(2,1)} %convert.35), channel_id=1, source_target_pairs={{0,5},{1,6},{2,7},{3,8},{4,9},{5,10},{6,11},{7,12},{8,13},{9,14},{... | collective-permute-start | bytes 18440
  770.0 348.6 %collective-permute-start.19 = (bf16[192,12]{0,1:T(8,128)(2,1)}, bf16[192,12]{0,1:T(8,128)(2,1)S(1)}, u32[]{:S(2)}, u32[]{:S(2)}) collective-permute-start(bf16[192,12]{0,1:T(8,128)(2,1)} %slice.107), channel_id=1, source_target_pairs={{0,16},{1,17},{2,18},{3,19},{4,20},{5,21},{6,22},{7,23},{8,24},{9,... | collective-permute-start | bytes 13832
  1118.6 20.3 %collective-permute-start.9 = (bf16[192,16]{0,1:T(8,128)(2,1)}, bf16[192,16]{0,1:T(8,128)(2,1)S(1)}, u32[]{:S(2)}, u32[]{:S(2)}) collective-permute-start(bf16[192,16]{0,1:T(8,128)(2,1)} %convert.35), channel_id=1, source_target_pairs={{0,6},{1,7},{2,8},{3,9},{4,10},{5,11},{6,12},{7,13},{8,14},{9,15},... | collective-permute-start | bytes 18440
  1121.2 19.6 %collective-permute-start.10 = (bf16[192,16]{0,1:T(8,128)(2,1)}, bf16[192,16]{0,1:T(8,128)(2,1)S(1)}, u32[]{:S(2)}, u32[]{:S(2)}) collective-permute-start(bf16[192,16]{0,1:T(8,128)(2,1)} %convert.35), channel_id=1, source_target_pairs={{0,7},{1,8},{2,9},{3,10},{4,11},{5,12},{6,13},{7,14},{8,15},{9,16}... | collective-permute-start | bytes 18440
  1122.5 27.2 %collective-permute-start.11 = (bf16[192,16]{0,1:T(8,128)(2,1)}, bf16[192,16]{0,1:T(8,128)(2,1)S(1)}, u32[]{:S(2)}, u32[]{:S(2)}) collective-permute-start(bf16[192,16]{0,1:T(8,128)(2,1)} %convert.35), channel_id=1, source_target_pairs={{0,8},{1,9},{2,10},{3,11},{4,12},{5,13},{6,14},{7,15},{8,16},{9,17... | collective-permute-start | bytes 18440
  1123.8 27.2 %collective-permute-start.12 = (bf16[192,16]{0,1:T(8,128)(2,1)}, bf16[192,16]{0,1:T(8,128)(2,1)S(1)}, u32[]{:S(2)}, u32[]{:S(2)}) collective-permute-start(bf16[192,16]{0,1:T(8,128)(2,1)} %convert.35), channel_id=1, source_target_pairs={{0,9},{1,10},{2,11},{3,12},{4,13},{5,14},{6,15},{7,16},{8,17},{9,1... | collective-permute-start | bytes 18440
  1132.6 20.1 %collective-permute-start.13 = (bf16[192,16]{0,1:T(8,128)(2,1)}, bf16[192,16]{0,1:T(8,128)(2,1)S(1)}, u32[]{:S(2)}, u32[]{:S(2)}) collective-permute-start(bf16[192,16]{0,1:T(8,128)(2,1)} %convert.35), channel_id=1, source_target_pairs={{0,10},{1,11},{2,12},{3,13},{4,14},{5,15},{6,16},{7,17},{8,18},{9,... | collective-permute-start | bytes 18440
  1138.9 17.8 %collective-permute-start.14 = (bf16[192,16]{0,1:T(8,128)(2,1)}, bf16[192,16]{0,1:T(8,128)(2,1)S(1)}, u32[]{:S(2)}, u32[]{:S(2)}) collective-permute-start(bf16[192,16]{0,1:T(8,128)(2,1)} %convert.35), channel_id=1, source_target_pairs={{0,11},{1,12},{2,13},{3,14},{4,15},{5,16},{6,17},{7,18},{8,19},{9,... | collective-permute-start | bytes 18440
  1140.8 19.1 %collective-permute-start.15 = (bf16[192,16]{0,1:T(8,128)(2,1)}, bf16[192,16]{0,1:T(8,128)(2,1)S(1)}, u32[]{:S(2)}, u32[]{:S(2)}) collective-permute-start(bf16[192,16]{0,1:T(8,128)(2,1)} %convert.35), channel_id=1, source_target_pairs={{0,12},{1,13},{2,14},{3,15},{4,16},{5,17},{6,18},{7,19},{8,20},{9,... | collective-permute-start | bytes 18440
  1149.7 10.2 collective-permute-start.16
  1151.0 8.9 collective-permute-start.17
  1152.7 7.2 collective-permute-start.18
  1156.8 3.1 collective-permute-start.4
  1165.2 231.3 %collective-permute-start.2 = (bf16[1,8,3,12,192]{4,3,2,1,0:T(8,128)(2,1)S(1)}, bf16[1,8,3,12,192]{4,3,2,1,0:T(8,128)(2,1)S(1)}, u32[]{:S(2)}, u32[]{:S(2)}) collective-permute-start(bf16[1,8,3,12,192]{4,3,2,1,0:T(8,128)(2,1)S(1)} %fusion.27), channel_id=1, source_target_pairs={{192,0},{0,64},{64,128},{128,192},{193,1},{1,65},{65,129},{129,193... | collective-permute-start | bytes 331784 | tf_op jit(solution)/shard_map/ppermute | solution.py:21
  1396.7 10.7 collective-permute-start.3
  (38 other events, 2590.7 us)
Sparse Core Ops, SparseCore 0:
  9.9 267.0 all-gather.6
  1165.3 225.9 all-reduce.11
